TPU v7x, 32 devices: a whole 2x2x4 slice. The times are simulated.
32 devices in a mesh: obs: 16 (over z, x, core), sp: 2 (over y).
Axes of the slice: x: 2, y: 2, z: 4, core: 2. Of those that a mesh axis runs over, the one named last changes fastest.
Arguments:
- descriptors: bfloat16 [16384, 512], P('obs'), may hold values from -10 to 10
- candidates: bfloat16 [8192, 512], P('obs'), may hold values from -10 to 10
- sparse_index: int32 [4096], replicated, may hold values from 0 to 8191, as said below
- targets: bfloat16 [16384], P('obs'), may hold values from -12 to 12
- regularizer: float32 [4096], replicated, may hold values from 0.25 to 1
Outputs:
- inverse: float32 [4096, 4096], P('sp', 'obs')
- weights: float32 [4096], P('sp')
Inputs may be any that keep to these rules, and one draw needn't show every extreme that they name: `sparse_index`: the 4096 indices are distinct.
All inputs are finite; a program needn't handle non-finite values.
Results may differ from a plain program's by a relative error of at most 0.012.
Values may be sent and summed in bfloat16 or wider, within the bound.
A program may use at most 128 MiB of HBM per device.

v0:
```python
import math
import jax
import jax.numpy as jnp
from jax import lax
from jax.sharding import PartitionSpec as P

epsilon = 1e-06


def unit_rows(row_block):
    values = row_block.astype(jnp.float32)
    return (values * lax.rsqrt(jnp.sum(values * values, axis=1, keepdims=True) + epsilon)).astype(
        jnp.bfloat16
    )


def kernel_block(normed, sparse):
    inner = lax.dot_general(
        normed, sparse, (((1,), (1,)), ((), ())), preferred_element_type=jnp.float32
    )
    scaled = inner * math.sqrt(normed.shape[1])
    squared = scaled * scaled
    return (squared * squared - 6.0 * squared + 3.0).astype(jnp.bfloat16)


def select_rows(candidate_units, wanted, cand_start):
    shifted = wanted - cand_start
    inside = (shifted >= 0) & (shifted < candidate_units.shape[0])
    picked = candidate_units[jnp.clip(shifted, 0, candidate_units.shape[0] - 1)].astype(jnp.float32)
    return picked * inside[:, None].astype(jnp.float32)


def first_iterate(system_part, row_scale, col_scale, on_diag):
    return (
        jnp.where(on_diag, 2.0 * row_scale[:, None], 0.0)
        - system_part * row_scale[:, None] * col_scale[None, :]
    )


def on_device(descriptors, candidates, sparse_index, targets, regularizer):
    obs_count = lax.axis_size("obs")
    sp_count = lax.axis_size("sp")
    obs_pos = lax.axis_index("obs")
    sp_pos = lax.axis_index("sp")
    sparse_count = sparse_index.shape[0]
    block_rows = sparse_count // sp_count
    tile_cols = sparse_count // obs_count
    rows_all = descriptors.shape[0] * obs_count
    normed = unit_rows(descriptors)
    candidate_units = unit_rows(candidates)
    cand_start = obs_pos * candidates.shape[0]
    all_sparse = lax.psum(
        select_rows(candidate_units, sparse_index, cand_start).astype(jnp.bfloat16), "obs"
    )
    full_kernel = kernel_block(normed, all_sparse)
    own_kernel = lax.dynamic_slice_in_dim(full_kernel, sp_pos * block_rows, block_rows, 1)
    gram_part = lax.psum_scatter(
        lax.dot_general(
            full_kernel, own_kernel, (((0,), (0,)), ((), ())), preferred_element_type=jnp.float32
        ),
        "obs",
        scatter_dimension=0,
        tiled=True,
    )
    weighted = jnp.dot(targets, own_kernel, preferred_element_type=jnp.float32)
    squares = jnp.sum(jnp.square(own_kernel.astype(jnp.float32)), axis=0)
    weighted, squares = lax.psum((weighted, squares), "obs")
    weighted, squares = (
        lax.all_gather(weighted, "sp", axis=0, tiled=True),
        lax.all_gather(squares, "sp", axis=0, tiled=True),
    )
    normalizer = 24.0 * rows_all
    projected = weighted / math.sqrt(normalizer)
    recip = 1.0 / (squares / normalizer + regularizer)
    row_ids = sp_pos * block_rows + lax.iota(jnp.int32, block_rows)
    col_ids = obs_pos * tile_cols + lax.iota(jnp.int32, tile_cols)
    all_ids = lax.iota(jnp.int32, sparse_count)
    on_diag = row_ids[:, None] == col_ids[None, :]
    reg_rows = lax.dynamic_slice_in_dim(regularizer, sp_pos * block_rows, block_rows)
    recip_rows = lax.dynamic_slice_in_dim(recip, sp_pos * block_rows, block_rows)
    recip_cols = lax.dynamic_slice_in_dim(recip, obs_pos * tile_cols, tile_cols)
    system_tile = gram_part.T / normalizer + jnp.where(on_diag, reg_rows[:, None], 0.0)
    highest = lax.Precision.HIGHEST
    system_full_rows = lax.all_gather(system_tile, "obs", axis=1, tiled=True)
    system_full_cols = lax.all_gather(system_tile, "sp", axis=0, tiled=True)
    first_rows = first_iterate(
        system_full_rows, recip_rows, recip, row_ids[:, None] == all_ids[None, :]
    )
    first_cols = first_iterate(
        system_full_cols, recip, recip_cols, all_ids[:, None] == col_ids[None, :]
    )
    product_tile = jnp.dot(system_full_rows, first_cols, precision=highest)
    product_full_cols = lax.all_gather(product_tile, "sp", axis=0, tiled=True)
    first_tile = first_iterate(system_tile, recip_rows, recip_cols, on_diag)
    inverse_tile = 2.0 * first_tile - jnp.dot(first_rows, product_full_cols, precision=highest)
    projected_cols = lax.dynamic_slice_in_dim(projected, obs_pos * tile_cols, tile_cols)
    weight_part = jnp.dot(inverse_tile, projected_cols, precision=highest)
    weights = lax.psum(weight_part, "obs")
    return (inverse_tile, weights)


def solution(mesh):
    in_specs = (P("obs", None), P("obs", None), P(), P("obs"), P())
    out_specs = (P("sp", "obs"), P("sp"))
    return jax.shard_map(
        on_device, mesh=mesh, in_specs=in_specs, out_specs=out_specs, check_vma=False
    )
```

profile of v0, /device:TPU:0, one launch (start us, length us, event | category | flops | bytes accessed | tf_op | source)
XLA Modules:
  0.0 955.4 jit_solution(15224427852561429307)
XLA Ops:
  7.2 0.0 all-reduce.3.cloned.1.call-start
  7.2 0.7 fusion.36
  7.9 0.7 and_convert_fusion
  8.7 1.2 fusion.32
  9.9 1.2 fusion.33
  11.1 17.3 %gather_fusion = bf16[4096,512]{1,0:T(8,128)(2,1)} fusion(bf16[512,512]{1,0:T(8,128)(2,1)S(1)} %fusion.33, s32[4096]{0:T(1024)S(1)} %fusion.36), kind=kCustom, calls=%fused_computation | custom fusion | bytes 8404992 | tf_op jit(solution)/shard_map/gather | solution.py:29
  28.4 4.0 multiply_convert_fusion
  32.5 0.0 copy-start.3
  32.5 0.0 all-reduce.3.cloned.1.call-update
  32.5 0.0 reduce-scatter.2.cloned.1.call-start
  32.6 1.1 copy-done.3
  33.7 0.3 fusion.22
  34.0 112.7 %all-reduce.3.cloned.1.call-done = bf16[4096,512]{1,0:T(8,128)(2,1)} async-done(((bf16[4096,512]{1,0:T(8,128)(2,1)}), bf16[4096,512]{1,0:T(8,128)(2,1)}) %all-reduce.3.cloned.1.call-update) | async-done | bytes 4194320 | tf_op jit(solution)/shard_map/psum | solution.py:52
  146.7 7.7 add_convert_fusion
  154.4 0.0 copy-start.2
  154.4 3.2 copy-done.2
  157.6 22.4 %fusion.17 = f32[4096,2048]{1,0:T(8,128)} fusion(bf16[1024,4096]{1,0:T(8,128)(2,1)S(1)} %add_convert_fusion, s32[]{:T(128)} %select_n.28), kind=kOutput, calls=%fused_computation.23 | convolution fusion | flops 17179869184 | bytes 46137348 | tf_op jit(solution)/shard_map/dot_general | solution.py:58
  180.0 0.0 dynamic-slice-start
  180.0 0.0 reduce-scatter.2.cloned.1.call-update
  180.1 0.0 all-gather.6.cloned.1.call-start
  180.1 0.0 copy-start.5
  180.2 331.8 %reduce-scatter.2.cloned.1.call-done = f32[256,2048]{1,0:T(8,128)} async-done(((f32[4096,2048]{1,0:T(8,128)}), f32[256,2048]{1,0:T(8,128)}) %reduce-scatter.2.cloned.1.call-update) | async-done | bytes 2097168 | tf_op jit(solution)/shard_map/reduce_scatter | solution.py:57
  512.0 0.0 dynamic-slice-done
  512.0 3.3 fusion.26
  515.2 0.0 all-gather.6.cloned.1.call-update
  515.3 0.0 all-gather.4.cloned.1.call-start
  515.3 0.5 all-gather.4.cloned.1.call-update
  515.9 0.0 all-gather.8.cloned.1.call-start
  515.9 0.0 copy-done.5
  515.9 0.0 copy-start.4
  515.9 3.1 multiply_reduce_fusion
  519.0 3.3 fusion.15
  522.3 59.1 %all-reduce = (f32[2048]{0:T(1024)S(1)}, f32[2048]{0:T(1024)S(1)}) all-reduce(f32[2048]{0:T(1024)S(1)} %multiply_reduce_fusion, f32[2048]{0:T(1024)S(1)} %bitcast.13), channel_id=1, replica_groups=mesh['obs'=16,'sp'=2] {'obs'}, use_global_device_ids=true, to_apply=%region_4.5 | all-reduce | flops 4096 | bytes 32768 | tf_op jit(solution)/shard_map/psum | solution.py:67
  581.4 4.4 all_gather.15
  585.7 0.0 copy-done.4
  585.7 0.1 dynamic_slice.18
  585.8 155.6 %all-gather.4.cloned.1.call-done = f32[2048,4096]{0,1:T(8,128)} async-done(((f32[2048,256]{0,1:T(8,128)}), f32[2048,4096]{0,1:T(8,128)}) %all-gather.4.cloned.1.call-update) | async-done | bytes 33554448 | tf_op jit(solution)/shard_map/all_gather | solution.py:84
  741.4 67.7 %fusion.10 = f32[2048,256]{1,0:T(8,128)} fusion(f32[2048,4096]{0,1:T(8,128)} %all-gather.4.cloned.1.call-done, f32[4096,256]{0,1:T(8,128)} %all-gather.6.cloned.1.call-done, f32[256]{0:T(256)S(1)} %dynamic_slice.18, f32[4096]{0:T(1024)S(1)} %get-tuple-element.11, f32[4096]{0:T(1024)S(1)} %get-tuple-element.10, s32[256]{0:T(256)S(1)} %iota_add_fusion.1), kind=kOutput, calls=%fused_computation.15 | convolution fusion | flops 25775046656 | bytes 39880704 | tf_op jit(solution)/shard_map/dot_general | solution.py:92
  809.1 0.0 all-gather.8.cloned.1.call-update
  809.1 4.4 all_gather.19
  813.4 0.1 dynamic-slice_multiply_fusion
  813.5 52.5 %all-gather.8.cloned.1.call-done = f32[4096,256]{1,0:T(8,128)} async-done(((f32[2048,256]{1,0:T(8,128)}), f32[4096,256]{1,0:T(8,128)}) %all-gather.8.cloned.1.call-update) | async-done | bytes 4194320 | tf_op jit(solution)/shard_map/all_gather | solution.py:93
  866.0 0.0 copy-done
  866.0 44.1 %fusion.19 = f32[2048,256]{0,1:T(8,128)} fusion(f32[4096,256]{1,0:T(8,128)} %all-gather.8.cloned.1.call-done, f32[2048,4096]{0,1:T(8,128)} %all-gather.4.cloned.1.call-done, f32[4096]{0:T(1024)S(1)} %get-tuple-element.11, f32[2048]{0:T(1024)S(1)} %get-tuple-element.9, f32[2048]{0:T(1024)S(1)} %get-tuple-element.8, s32[2048]{0:T(1024)S(1)} %iota_add_fusion, ...), kind=kOutput, calls=%fused_computation.25 | convolution fusion | flops 25815416832 | bytes 41986048 | tf_op jit(solution)/shard_map/dot_general | solution.py:95
  910.1 3.0 copy.10
  913.1 0.0 copy-done.1
  913.1 1.2 fusion.41
  914.3 34.2 %psum.31 = f32[2048]{0:T(1024)} all-reduce(f32[2048]{0:T(1024)S(1)} %bitcast.12), channel_id=1, replica_groups=mesh['obs'=16,'sp'=2] {'obs'}, use_global_device_ids=true, to_apply=%region_7.8 | all-reduce | flops 2048 | bytes 16384 | tf_op jit(solution)/shard_map/psum | solution.py:98
  (10 shorter events, 0.0 us)
Async XLA Ops:
  7.2 139.6 %all-reduce.3.cloned.1.call-start = ((), (), s32[]{:S(2)}) async-start(), calls=%async_computation.1 | async-start | bytes 8388608 | tf_op jit(solution)/shard_map/psum | solution.py:52
  32.5 1.2 copy-start.3
  32.5 479.5 %reduce-scatter.2.cloned.1.call-start = ((), (), s32[]{:S(2)}) async-start(), calls=%async_computation.2 | async-start | bytes 35651584 | tf_op jit(solution)/shard_map/reduce_scatter | solution.py:57
  154.4 3.2 copy-start.2
  180.0 331.9 %dynamic-slice-start = ((f32[4096]{0:T(1024)}, s32[]{:T(128)}), f32[2048]{0:T(1024)S(1)}, s32[]{:S(2)}) async-start(f32[4096]{0:T(1024)} %param.9, s32[]{:T(128)} %select_n.28), calls=%async_computation.6 | async-start | bytes 16896 | tf_op jit(solution)/shard_map/dynamic_slice | solution.py:79
  180.1 405.7 %all-gather.6.cloned.1.call-start = ((), (), s32[]{:S(2)}) async-start(), calls=%async_computation.4 | async-start | bytes 6291456 | tf_op jit(solution)/shard_map/all_gather | solution.py:85
  180.1 335.8 %copy-start.5 = (bf16[1024]{0:T(1024)(128)(2,1)S(1)}, bf16[1024]{0:T(1024)(128)(2,1)}, u32[]{:S(2)}) copy-start(bf16[1024]{0:T(1024)(128)(2,1)} %param.8) | copy-start | bytes 6148
  515.3 226.1 %all-gather.4.cloned.1.call-start = ((), (), s32[]{:S(2)}) async-start(), calls=%async_computation.3 | async-start | bytes 35651584 | tf_op jit(solution)/shard_map/all_gather | solution.py:84
  515.9 350.1 %all-gather.8.cloned.1.call-start = ((), (), s32[]{:S(2)}) async-start(), calls=%async_computation.5 | async-start | bytes 6291456 | tf_op jit(solution)/shard_map/all_gather | solution.py:93
  515.9 69.8 %copy-start.4 = (f32[4096]{0:T(1024)S(1)}, f32[4096]{0:T(1024)}, u32[]{:S(2)}) copy-start(f32[4096]{0:T(1024)} %param.9) | copy-start | bytes 49156
  741.4 124.6 %copy-start = (f32[2048,256]{0,1:T(8,128)S(1)}, f32[2048,256]{0,1:T(8,128)}, u32[]{:S(2)}) copy-start(f32[2048,256]{0,1:T(8,128)} %fusion.26) | copy-start | bytes 6291460
  910.1 3.0 copy-start.1
Sparse Core Ops, SparseCore 0:
  32.6 114.0 all-reduce.2
  180.2 331.7 reduce-scatter.1
  515.4 55.7 all-gather.5
  573.3 168.0 all-gather.3
  809.2 56.7 all-gather.7
where the time goes:
time: 964 us; the launch traced here: 955 us
  waiting for transfers between devices  653 us (68%)
  matrix products  146 us (15%)
  blocking collectives  102 us (11%)
  local copies, waits for them, and re-layouts  24.8 us (3%)
  other arithmetic  14.6 us (2%)
  between operations  14.3 us (1%)
    reduce_scatter x1, waiting for transfers between devices, on_device(): lax.psum_scatter(lax.dot_general(full_kernel, own_kernel, (((0,), (0,)),...  332 us
    all_gather x1, waiting for transfers between devices, on_device(): system_full_rows = lax.all_gather(system_tile, 'obs', axis=1, tiled=True)  156 us
    psum x1, waiting for transfers between devices, on_device(): lax.psum(select_rows(candidate_units, sparse_index, cand_start).astype(jn...  113 us
    dot_general x1, matrix products, on_device(): product_tile = jnp.dot(system_full_rows, first_cols, precision=highest)  67.7 us
    psum x1, blocking collectives, on_device(): weighted, squares = lax.psum((weighted, squares), 'obs')  59.1 us
    all_gather x1, waiting for transfers between devices, on_device(): product_full_cols = lax.all_gather(product_tile, 'sp', axis=0, tiled=True)  52.5 us
    dot_general x1, matrix products, on_device(): jnp.dot(first_rows, product_full_cols, precision=highest)  44.1 us
    psum x1, blocking collectives, on_device(): weights = lax.psum(weight_part, 'obs')  34.2 us
  transfers between devices with their start and end apart: 5, of which 4 were waited for; matrix products, arithmetic and copies ran while one was open for 1% of the time, Pallas kernels for 0%

commit v1 on v0

--- a/solution.py
+++ b/solution.py
@@ -49,8 +49,11 @@
     normed = unit_rows(descriptors)
     candidate_units = unit_rows(candidates)
     cand_start = obs_pos * candidates.shape[0]
-    all_sparse = lax.psum(
-        select_rows(candidate_units, sparse_index, cand_start).astype(jnp.bfloat16), "obs"
+    all_sparse = jnp.sum(
+        lax.all_gather(
+            select_rows(candidate_units, sparse_index, cand_start).astype(jnp.bfloat16), "obs"
+        ),
+        axis=0,
     )
     full_kernel = kernel_block(normed, all_sparse)
     own_kernel = lax.dynamic_slice_in_dim(full_kernel, sp_pos * block_rows, block_rows, 1)

time: 964 us -> 1200 us (1.24)
  waiting for transfers between devices: 653 us -> 869 us
  other arithmetic: 14.6 us -> 38.3 us
    all_gather x0 -> x1, waiting for transfers between devices: none -> 327 us  [on_device(): lax.all_gather(select_rows(candidate_units, sparse_index, cand_start).ast...]
    psum x1 -> x0, waiting for transfers between devices: 113 us -> none  [on_device(): lax.psum(select_rows(candidate_units, sparse_index, cand_start).astype(jn...]
    reduce_sum x0 -> x1, other arithmetic: none -> 23.7 us  [on_device(): jnp.sum(lax.all_gather(select_rows(candidate_units, sparse_index, cand_st...]
where the time goes in v1:
time: 1200 us; the launch traced here: 1190 us
  waiting for transfers between devices  869 us (72%)
  matrix products  146 us (12%)
  blocking collectives  102 us (8%)
  other arithmetic  38.3 us (3%)
  local copies, waits for them, and re-layouts  24.8 us (2%)
  between operations  14.3 us (1%)
    reduce_scatter x1, waiting for transfers between devices, on_device(): lax.psum_scatter(lax.dot_general(full_kernel, own_kernel, (((0,), (0,)),...  333 us
    all_gather x1, waiting for transfers between devices, on_device(): lax.all_gather(select_rows(candidate_units, sparse_index, cand_start).ast...  327 us
    all_gather x1, waiting for transfers between devices, on_device(): system_full_rows = lax.all_gather(system_tile, 'obs', axis=1, tiled=True)  155 us
    dot_general x1, matrix products, on_device(): product_tile = jnp.dot(system_full_rows, first_cols, precision=highest)  67.7 us
    psum x1, blocking collectives, on_device(): weighted, squares = lax.psum((weighted, squares), 'obs')  59.2 us
    all_gather x1, waiting for transfers between devices, on_device(): product_full_cols = lax.all_gather(product_tile, 'sp', axis=0, tiled=True)  52.5 us
    dot_general x1, matrix products, on_device(): jnp.dot(first_rows, product_full_cols, precision=highest)  44.1 us
    psum x1, blocking collectives, on_device(): weights = lax.psum(weight_part, 'obs')  34.2 us
  transfers between devices with their start and end apart: 5, of which 4 were waited for; matrix products, arithmetic and copies ran while one was open for 1% of the time, Pallas kernels for 0%

profile of v1, /device:TPU:0, one launch (start us, length us, event | category | flops | bytes accessed | tf_op | source)
XLA Modules:
  0.0 1194.6 jit_solution(12440192629246548952)
XLA Ops:
  7.2 0.0 all-gather.5.cloned.1.call-start
  7.2 0.7 fusion.37
  7.9 0.7 and_convert_fusion
  8.7 1.2 fusion.33
  9.9 1.2 fusion.34
  11.1 17.3 %gather_fusion = bf16[4096,512]{1,0:T(8,128)(2,1)} fusion(bf16[512,512]{1,0:T(8,128)(2,1)S(1)} %fusion.34, s32[4096]{0:T(1024)S(1)} %fusion.37), kind=kCustom, calls=%fused_computation | custom fusion | bytes 8404992 | tf_op jit(solution)/shard_map/gather | solution.py:29
  28.4 4.0 fusion.10
  32.4 0.0 copy-start.3
  32.4 0.0 all-gather.5.cloned.1.call-update
  32.5 0.0 reduce-scatter.2.cloned.1.call-start
  32.5 1.1 copy-done.3
  33.7 0.3 fusion.23
  33.9 327.5 %all-gather.5.cloned.1.call-done = bf16[16,4096,512]{2,1,0:T(8,128)(2,1)} async-done(((bf16[1,4096,512]{2,1,0:T(8,128)(2,1)}), bf16[16,4096,512]{2,1,0:T(8,128)(2,1)}) %all-gather.5.cloned.1.call-update) | async-done | bytes 67108880 | tf_op jit(solution)/shard_map/all_gather | solution.py:53
  361.4 23.7 %reduce_sum.41 = bf16[4096,512]{1,0:T(8,128)(2,1)} reduce(bf16[16,4096,512]{2,1,0:T(8,128)(2,1)} %all-gather.5.cloned.1.call-done, bf16[]{:T(256)} %constant.11.clone.1), dimensions={0}, to_apply=%region_2.3 | reduce | flops 31457280 | bytes 71303168 | tf_op jit(solution)/shard_map/reduce_sum | solution.py:52
  385.1 7.7 add_convert_fusion
  392.8 0.0 copy-start.2
  392.8 3.2 copy-done.2
  396.0 22.4 %fusion.18 = f32[4096,2048]{1,0:T(8,128)} fusion(bf16[1024,4096]{1,0:T(8,128)(2,1)S(1)} %add_convert_fusion, s32[]{:T(128)} %select_n.28), kind=kOutput, calls=%fused_computation.24 | convolution fusion | flops 17179869184 | bytes 46137348 | tf_op jit(solution)/shard_map/dot_general | solution.py:61
  418.4 0.0 reduce-scatter.2.cloned.1.call-update
  418.4 0.0 all-gather.9.cloned.1.call-start
  418.5 0.0 copy-start.5
  418.5 332.7 %reduce-scatter.2.cloned.1.call-done = f32[256,2048]{1,0:T(8,128)} async-done(((f32[4096,2048]{1,0:T(8,128)}), f32[256,2048]{1,0:T(8,128)}) %reduce-scatter.2.cloned.1.call-update) | async-done | bytes 2097168 | tf_op jit(solution)/shard_map/reduce_scatter | solution.py:60
  751.2 0.0 dynamic-slice-done
  751.2 3.3 fusion.27
  754.4 0.0 all-gather.9.cloned.1.call-update
  754.4 0.0 all-gather.7.cloned.1.call-start
  754.5 0.5 all-gather.7.cloned.1.call-update
  755.0 0.0 all-gather.11.cloned.1.call-start
  755.1 0.0 copy-done.5
  755.1 0.0 copy-start.4
  755.1 3.1 multiply_reduce_fusion
  758.2 3.3 fusion.16
  761.4 59.2 %all-reduce = (f32[2048]{0:T(1024)S(1)}, f32[2048]{0:T(1024)S(1)}) all-reduce(f32[2048]{0:T(1024)S(1)} %multiply_reduce_fusion, f32[2048]{0:T(1024)S(1)} %bitcast.16), channel_id=1, replica_groups=mesh['obs'=16,'sp'=2] {'obs'}, use_global_device_ids=true, to_apply=%region_4.5 | all-reduce | flops 4096 | bytes 32768 | tf_op jit(solution)/shard_map/psum | solution.py:70
  820.6 4.4 all_gather.20
  825.0 0.0 copy-done.4
  825.0 0.1 dynamic_slice.18
  825.1 155.5 %all-gather.7.cloned.1.call-done = f32[2048,4096]{0,1:T(8,128)} async-done(((f32[2048,256]{0,1:T(8,128)}), f32[2048,4096]{0,1:T(8,128)}) %all-gather.7.cloned.1.call-update) | async-done | bytes 33554448 | tf_op jit(solution)/shard_map/all_gather | solution.py:87
  980.5 67.7 %fusion.11 = f32[2048,256]{1,0:T(8,128)} fusion(f32[2048,4096]{0,1:T(8,128)} %all-gather.7.cloned.1.call-done, f32[4096,256]{0,1:T(8,128)} %all-gather.9.cloned.1.call-done, f32[256]{0:T(256)S(1)} %dynamic_slice.18, f32[4096]{0:T(1024)S(1)} %get-tuple-element.11, f32[4096]{0:T(1024)S(1)} %get-tuple-element.10, s32[256]{0:T(256)S(1)} %iota_add_fusion.1), kind=kOutput, calls=%fused_computation.16 | convolution fusion | flops 25775046656 | bytes 39880704 | tf_op jit(solution)/shard_map/dot_general | solution.py:95
  1048.2 0.0 all-gather.11.cloned.1.call-update
  1048.2 4.4 all_gather.24
  1052.6 0.1 dynamic-slice_multiply_fusion
  1052.7 52.5 %all-gather.11.cloned.1.call-done = f32[4096,256]{1,0:T(8,128)} async-done(((f32[2048,256]{1,0:T(8,128)}), f32[4096,256]{1,0:T(8,128)}) %all-gather.11.cloned.1.call-update) | async-done | bytes 4194320 | tf_op jit(solution)/shard_map/all_gather | solution.py:96
  1105.1 0.0 copy-done
  1105.1 44.1 %fusion.20 = f32[2048,256]{0,1:T(8,128)} fusion(f32[4096,256]{1,0:T(8,128)} %all-gather.11.cloned.1.call-done, f32[2048,4096]{0,1:T(8,128)} %all-gather.7.cloned.1.call-done, f32[4096]{0:T(1024)S(1)} %get-tuple-element.11, f32[2048]{0:T(1024)S(1)} %get-tuple-element.9, f32[2048]{0:T(1024)S(1)} %get-tuple-element.8, s32[2048]{0:T(1024)S(1)} %iota_add_fusion, ...), kind=kOutput, calls=%fused_computation.26 | convolution fusion | flops 25815416832 | bytes 41986048 | tf_op jit(solution)/shard_map/dot_general | solution.py:98
  1149.2 3.0 copy.10
  1152.2 0.0 copy-done.1
  1152.2 1.2 fusion.42
  1153.4 34.2 %psum.23 = f32[2048]{0:T(1024)} all-reduce(f32[2048]{0:T(1024)S(1)} %bitcast.15), channel_id=1, replica_groups=mesh['obs'=16,'sp'=2] {'obs'}, use_global_device_ids=true, to_apply=%region_7.8 | all-reduce | flops 2048 | bytes 16384 | tf_op jit(solution)/shard_map/psum | solution.py:101
  (11 shorter events, 0.0 us)
Async XLA Ops:
  7.2 354.2 %all-gather.5.cloned.1.call-start = ((), (), s32[]{:S(2)}) async-start(), calls=%async_computation.1 | async-start | bytes 71303168 | tf_op jit(solution)/shard_map/all_gather | solution.py:53
  32.4 1.2 copy-start.3
  32.5 718.7 %reduce-scatter.2.cloned.1.call-start = ((), (), s32[]{:S(2)}) async-start(), calls=%async_computation.2 | async-start | bytes 35651584 | tf_op jit(solution)/shard_map/reduce_scatter | solution.py:60
  392.8 3.2 copy-start.2
  418.4 332.8 %dynamic-slice-start = ((f32[4096]{0:T(1024)}, s32[]{:T(128)}), f32[2048]{0:T(1024)S(1)}, s32[]{:S(2)}) async-start(f32[4096]{0:T(1024)} %param.9, s32[]{:T(128)} %select_n.28), calls=%async_computation.6 | async-start | bytes 16896 | tf_op jit(solution)/shard_map/dynamic_slice | solution.py:82
  418.4 406.6 %all-gather.9.cloned.1.call-start = ((), (), s32[]{:S(2)}) async-start(), calls=%async_computation.4 | async-start | bytes 6291456 | tf_op jit(solution)/shard_map/all_gather | solution.py:88
  418.5 336.6 %copy-start.5 = (bf16[1024]{0:T(1024)(128)(2,1)S(1)}, bf16[1024]{0:T(1024)(128)(2,1)}, u32[]{:S(2)}) copy-start(bf16[1024]{0:T(1024)(128)(2,1)} %param.8) | copy-start | bytes 6148
  754.4 226.1 %all-gather.7.cloned.1.call-start = ((), (), s32[]{:S(2)}) async-start(), calls=%async_computation.3 | async-start | bytes 35651584 | tf_op jit(solution)/shard_map/all_gather | solution.py:87
  755.0 350.1 %all-gather.11.cloned.1.call-start = ((), (), s32[]{:S(2)}) async-start(), calls=%async_computation.5 | async-start | bytes 6291456 | tf_op jit(solution)/shard_map/all_gather | solution.py:96
  755.1 69.9 %copy-start.4 = (f32[4096]{0:T(1024)S(1)}, f32[4096]{0:T(1024)}, u32[]{:S(2)}) copy-start(f32[4096]{0:T(1024)} %param.9) | copy-start | bytes 49156
  980.5 124.6 %copy-start = (f32[2048,256]{0,1:T(8,128)S(1)}, f32[2048,256]{0,1:T(8,128)}, u32[]{:S(2)}) copy-start(f32[2048,256]{0,1:T(8,128)} %fusion.27) | copy-start | bytes 6291460
  1149.2 3.0 copy-start.1
Sparse Core Ops, SparseCore 0:
  32.6 328.7 all-gather.4
  418.5 332.5 reduce-scatter.1
  754.6 55.8 all-gather.8
  812.4 168.0 all-gather.6
  1048.4 56.7 all-gather.10
